TPU v7x, 256 devices: a whole 4x4x8 slice. The times are simulated.
256 devices in a mesh: space: 32 (over x, y, core), tm: 8 (over z).
Axes of the slice: x: 4, y: 4, z: 8, core: 2. Of those that a mesh axis runs over, the one named last changes fastest.
Arguments:
- velocity: bfloat16 [256, 2, 512, 1024], P('tm', None, 'space'), may hold values from -8.4 to 8.4
Outputs:
- vorticity: bfloat16 [256, 512, 1024], P('tm', 'space')
- modes: float32 [32, 512, 1024], P('tm', 'space')
All inputs are finite; a program needn't handle non-finite values.
Results may differ from a plain program's by a relative error of at most 0.003.
Values may be sent and summed in bfloat16 or wider, within the bound.
A program may use at most 64 MiB of HBM per device.

v0:
```python
import jax
import jax.numpy as jnp
from jax import lax
from jax.sharding import PartitionSpec as P

RANK = 32


def extended(block, sides, width):
    for axis, dim in sides:
        count = lax.axis_size(axis)
        forward = [(i, i + 1) for i in range(count - 1)]
        forward.append((count - 1, 0))
        backward = [(target, source) for source, target in forward]
        low = lax.ppermute(
            lax.slice_in_dim(block, block.shape[dim] - width, None, axis=dim), axis, forward
        )
        high = lax.ppermute(lax.slice_in_dim(block, 0, width, axis=dim), axis, backward)
        block = jnp.concatenate([low, block, high], axis=dim)
    return block


def partner_2(value, axis, apart):
    mask = 2**apart
    pairs = [(source, source ^ mask) for source in range(lax.axis_size(axis))]
    return lax.ppermute(value, axis, pairs)


def merge_nodes(stacked):
    high = lax.Precision.HIGHEST
    gram = lax.psum(jnp.einsum("naxz,nbxz->nab", stacked, stacked, precision=high), "space")
    coeffs = gram[:, :, :RANK] + gram[:, :, RANK:]
    diagonal = jnp.diagonal(gram, axis1=1, axis2=2)
    scales = jnp.sqrt(diagonal[:, :RANK] + diagonal[:, RANK:])
    eye = jnp.broadcast_to(jnp.eye(RANK, dtype=jnp.float32), (stacked.shape[0], RANK, RANK))
    mixed = jnp.einsum("nab,naxz->nbxz", coeffs, stacked, precision=high)
    inner = lax.psum(jnp.einsum("naxz,nbxz->nab", mixed, mixed, precision=high), "space")
    lower = jnp.linalg.cholesky(inner)
    lower_inv = lax.linalg.triangular_solve(lower, eye, left_side=True, lower=True)
    factor = jnp.swapaxes(lower_inv, 1, 2) * scales[:, None, :]
    return jnp.einsum("nab,naxz->nbxz", factor, mixed, precision=high)


def spanwise(field):
    ahead = jnp.roll(field, -1, 2)
    behind = jnp.roll(field, 1, 2)
    ahead_two = jnp.roll(field, -2, 2)
    behind_two = jnp.roll(field, 2, 2)
    return (8.0 * (ahead - behind) - (ahead_two - behind_two)) / 12.0


def local(velocity):
    rows = velocity.shape[2]
    padded = extended(velocity, (("space", 2),), 2).astype(jnp.float32)
    stream_u = padded[:, 0, 2 : rows + 2]
    span_v = padded[:, 1]
    dv_dx = (
        8.0 * (span_v[:, 3 : rows + 3] - span_v[:, 1 : rows + 1])
        - (span_v[:, 4:] - span_v[:, :rows])
    ) / 12.0
    vorticity = (dv_dx - spanwise(stream_u)).astype(jnp.bfloat16)
    blocks = lax.axis_size("tm")
    levels = blocks.bit_length() - 1
    my_block = lax.axis_index("tm")
    share = RANK // blocks
    fields = vorticity.astype(jnp.float32)
    for level in range(levels):
        if level == 0:
            partner = partner_2(vorticity, "tm", 0).astype(jnp.float32)
        else:
            partner = partner_2(fields, "tm", level)
        upper = my_block // 2**level % 2 == 1
        first = jnp.where(upper, partner, fields)
        second = jnp.where(upper, fields, partner)
        fields = merge_nodes(jnp.concatenate([first, second], axis=0)[None])[0]
    modes = lax.dynamic_slice_in_dim(fields, my_block * share, share, 0)
    return (vorticity, modes)


def solution(mesh):
    in_specs = (P("tm", None, "space", None),)
    out_specs = (P("tm", "space", None), P("tm", "space", None))
    return jax.shard_map(local, mesh=mesh, in_specs=in_specs, out_specs=out_specs, check_vma=False)
```

profile of v0, /device:TPU:0, one launch (start us, length us, event | category | flops | bytes accessed | tf_op | source)
XLA Modules:
  0.0 1045.1 jit_solution(1491497612664828559)
XLA Ops:
  0.6 2.7 copy.17
  3.4 3.0 collective-permute-start.1
  6.4 3.9 collective-permute-done.1
  10.3 5.2 collective-permute-done
  18.1 2.4 fusion.9
  22.5 15.7 %collective-permute-done.2 = bf16[32,16,1024]{2,0,1:T(8,128)(2,1)S(1)} collective-permute-done((bf16[32,16,1024]{2,0,1:T(8,128)(2,1)S(1)}, bf16[32,16,1024]{2,0,1:T(8,128)(2,1)S(1)}, u32[]{:S(2)}, u32[]{:S(2)}) %collective-permute-start.2) | collective-permute-done | bytes 1048608 | tf_op jit(solution)/shard_map/ppermute | solution.py:26
  40.8 3.4 fusion.14
  44.2 129.4 %psum.42 = f32[1,64,64]{2,1,0:T(8,128)S(1)} all-reduce(f32[1,64,64]{2,1,0:T(8,128)S(1)} %fusion.14), channel_id=1, replica_groups=mesh['space'=32,'tm'=8] {'space'}, use_global_device_ids=true, to_apply=%region_0.1 | all-reduce | flops 4096 | bytes 32768 | tf_op jit(solution)/shard_map/psum | solution.py:31
  173.6 4.2 fusion.4
  179.6 123.8 %psum.43 = f32[1,32,32]{1,2,0:T(8,128)S(1)} all-reduce(f32[1,32,32]{1,2,0:T(8,128)S(1)} %convolution_bitcast_fusion.5), channel_id=1, replica_groups=mesh['space'=32,'tm'=8] {'space'}, use_global_device_ids=true, to_apply=%region_1.2 | all-reduce | flops 1024 | bytes 8192 | tf_op jit(solution)/shard_map/psum | solution.py:37
  303.5 2.9 custom-call.16
  307.7 2.4 custom-call.17
  311.3 3.3 fusion.62
  314.6 3.3 collective-permute-start.3
  317.8 85.8 %collective-permute-done.3 = f32[32,16,1024]{2,0,1:T(8,128)S(1)} collective-permute-done((f32[32,16,1024]{2,0,1:T(8,128)}, f32[32,16,1024]{2,0,1:T(8,128)S(1)}, u32[]{:S(2)}, u32[]{:S(2)}) %collective-permute-start.3) | collective-permute-done | bytes 2097184 | tf_op jit(solution)/shard_map/ppermute | solution.py:26
  403.6 2.1 broadcast_select_fusion.1
  407.8 3.4 fusion.15
  411.2 125.6 %psum.44 = f32[1,64,64]{2,1,0:T(8,128)S(1)} all-reduce(f32[1,64,64]{2,1,0:T(8,128)S(1)} %fusion.15), channel_id=1, replica_groups=mesh['space'=32,'tm'=8] {'space'}, use_global_device_ids=true, to_apply=%region_4.7 | all-reduce | flops 4096 | bytes 32768 | tf_op jit(solution)/shard_map/psum | solution.py:31
  536.8 4.2 fusion.2
  542.8 123.8 %psum.45 = f32[1,32,32]{1,2,0:T(8,128)S(1)} all-reduce(f32[1,32,32]{1,2,0:T(8,128)S(1)} %convolution_bitcast_fusion.3), channel_id=1, replica_groups=mesh['space'=32,'tm'=8] {'space'}, use_global_device_ids=true, to_apply=%region_5.8 | all-reduce | flops 1024 | bytes 8192 | tf_op jit(solution)/shard_map/psum | solution.py:37
  666.6 2.9 custom-call.18
  670.9 2.4 custom-call.19
  674.4 3.3 fusion.63
  677.7 6.8 collective-permute-start.4
  686.1 85.1 %collective-permute-done.4 = f32[32,16,1024]{2,0,1:T(8,128)S(1)} collective-permute-done((f32[32,16,1024]{2,0,1:T(8,128)}, f32[32,16,1024]{2,0,1:T(8,128)S(1)}, u32[]{:S(2)}, u32[]{:S(2)}) %collective-permute-start.4) | collective-permute-done | bytes 2097184 | tf_op jit(solution)/shard_map/ppermute | solution.py:26
  771.2 2.1 broadcast_select_fusion.3
  775.3 3.4 fusion.16
  778.7 125.6 %psum.46 = f32[1,64,64]{2,1,0:T(8,128)S(1)} all-reduce(f32[1,64,64]{2,1,0:T(8,128)S(1)} %fusion.16), channel_id=1, replica_groups=mesh['space'=32,'tm'=8] {'space'}, use_global_device_ids=true, to_apply=%region_6.9 | all-reduce | flops 4096 | bytes 32768 | tf_op jit(solution)/shard_map/psum | solution.py:31
  904.4 4.2 fusion
  910.3 123.8 %psum.47 = f32[1,32,32]{1,2,0:T(8,128)S(1)} all-reduce(f32[1,32,32]{1,2,0:T(8,128)S(1)} %convolution_bitcast_fusion.1), channel_id=1, replica_groups=mesh['space'=32,'tm'=8] {'space'}, use_global_device_ids=true, to_apply=%region_7.10 | all-reduce | flops 1024 | bytes 8192 | tf_op jit(solution)/shard_map/psum | solution.py:37
  1034.2 2.9 custom-call.20
  1038.5 2.4 custom-call.21
  (55 shorter events, 28.3 us)
Async XLA Ops:
  3.4 6.9 collective-permute-start.1
  6.4 9.1 collective-permute-start
  20.5 17.7 %collective-permute-start.2 = (bf16[32,16,1024]{2,0,1:T(8,128)(2,1)S(1)}, bf16[32,16,1024]{2,0,1:T(8,128)(2,1)S(1)}, u32[]{:S(2)}, u32[]{:S(2)}) collective-permute-start(bf16[32,16,1024]{2,0,1:T(8,128)(2,1)S(1)} %fusion.9), channel_id=1, source_target_pairs={{0,1},{1,0},{2,3},{3,2},{4,5},{5,4},{6,7},{7,6},{8,9},{9,8},{10,11... | collective-permute-start | bytes 3145736 | tf_op jit(solution)/shard_map/ppermute | solution.py:26
  38.8 1.3 copy-start
  38.8 2.0 copy-start.1
  314.6 89.1 %collective-permute-start.3 = (f32[32,16,1024]{2,0,1:T(8,128)}, f32[32,16,1024]{2,0,1:T(8,128)S(1)}, u32[]{:S(2)}, u32[]{:S(2)}) collective-permute-start(f32[32,16,1024]{2,0,1:T(8,128)} %fusion.62), channel_id=1, source_target_pairs={{0,2},{1,3},{2,0},{3,1},{4,6},{5,7},{6,4},{7,5},{8,10},{9,11},{10,... | collective-permute-start | bytes 6291464 | tf_op jit(solution)/shard_map/ppermute | solution.py:26
  405.8 1.3 copy-start.2
  405.8 2.0 copy-start.3
  677.7 93.5 %collective-permute-start.4 = (f32[32,16,1024]{2,0,1:T(8,128)}, f32[32,16,1024]{2,0,1:T(8,128)S(1)}, u32[]{:S(2)}, u32[]{:S(2)}) collective-permute-start(f32[32,16,1024]{2,0,1:T(8,128)} %fusion.63), channel_id=1, source_target_pairs={{0,4},{1,5},{2,6},{3,7},{4,0},{5,1},{6,2},{7,3},{8,12},{9,13},{10,... | collective-permute-start | bytes 6291464 | tf_op jit(solution)/shard_map/ppermute | solution.py:26
  773.3 1.3 copy-start.4
  773.3 2.0 copy-start.5
where the time goes:
time: 1050 us
  blocking collectives  752 us (72%)
  waiting for transfers between devices  196 us (19%)
  matrix products  37.2 us (4%)
  other arithmetic  28.1 us (3%)
  local copies, waits for them, and re-layouts  15.8 us (2%)
  starting transfers between devices  15.1 us (1%)
    psum x3, blocking collectives, merge_nodes(): lax.psum(jnp.einsum('naxz,nbxz->nab', stacked, stacked, precision=high),...  381 us
    psum x3, blocking collectives, merge_nodes(): lax.psum(jnp.einsum('naxz,nbxz->nab', mixed, mixed, precision=high), 'spa...  371 us
    ppermute x3, waiting for transfers between devices, partner_2(): return lax.ppermute(value, axis, pairs)  187 us
  transfers between devices with their start and end apart: 5, of which 5 were waited for; matrix products, arithmetic and copies ran while one was open for 0% of the time, Pallas kernels for 0%

commit v1 on v0

--- a/solution.py
+++ b/solution.py
@@ -28,7 +28,10 @@
 
 def merge_nodes(stacked):
     high = lax.Precision.HIGHEST
-    gram = lax.psum(jnp.einsum("naxz,nbxz->nab", stacked, stacked, precision=high), "space")
+    gram = jnp.sum(
+        lax.all_gather(jnp.einsum("naxz,nbxz->nab", stacked, stacked, precision=high), "space"),
+        axis=0,
+    )
     coeffs = gram[:, :, :RANK] + gram[:, :, RANK:]
     diagonal = jnp.diagonal(gram, axis1=1, axis2=2)
     scales = jnp.sqrt(diagonal[:, :RANK] + diagonal[:, RANK:])

time: 1050 us -> 744 us (0.71)
  blocking collectives: 752 us -> 449 us
    psum x3 -> x0, blocking collectives: 381 us -> none  [merge_nodes(): lax.psum(jnp.einsum('naxz,nbxz->nab', stacked, stacked, precision=high),...]
    all_gather x0 -> x3, blocking collectives: none -> 69.4 us  [merge_nodes(): lax.all_gather(jnp.einsum('naxz,nbxz->nab', stacked, stacked, precision=h...]
where the time goes in v1:
time: 744 us; the launch traced here: 736 us
  blocking collectives  449 us (60%)
  waiting for transfers between devices  196 us (26%)
  matrix products  37.3 us (5%)
  other arithmetic  28.4 us (4%)
  starting transfers between devices  15.3 us (2%)
  local copies, waits for them, and re-layouts  9.89 us (1%)
    psum x3, blocking collectives, merge_nodes(): lax.psum(jnp.einsum('naxz,nbxz->nab', mixed, mixed, precision=high), 'spa...  379 us
    ppermute x3, waiting for transfers between devices, partner_2(): return lax.ppermute(value, axis, pairs)  186 us
    all_gather x3, blocking collectives, merge_nodes(): lax.all_gather(jnp.einsum('naxz,nbxz->nab', stacked, stacked, precision=h...  69.4 us
  transfers between devices with their start and end apart: 5, of which 5 were waited for; matrix products, arithmetic and copies ran while one was open for 0% of the time, Pallas kernels for 0%

profile of v1, /device:TPU:0, one launch (start us, length us, event | category | flops | bytes accessed | tf_op | source)
XLA Modules:
  0.0 736.4 jit_solution(6802546023524892588)
XLA Ops:
  0.6 2.7 copy.42
  3.4 3.0 collective-permute-start.1
  6.4 3.9 collective-permute-done.1
  10.3 5.2 collective-permute-done
  18.1 2.4 fusion.9
  22.5 15.7 %collective-permute-done.2 = bf16[32,16,1024]{2,0,1:T(8,128)(2,1)S(1)} collective-permute-done((bf16[32,16,1024]{2,0,1:T(8,128)(2,1)S(1)}, bf16[32,16,1024]{2,0,1:T(8,128)(2,1)S(1)}, u32[]{:S(2)}, u32[]{:S(2)}) %collective-permute-start.2) | collective-permute-done | bytes 1048608 | tf_op jit(solution)/shard_map/ppermute | solution.py:26
  38.9 3.4 fusion.14
  42.3 25.4 %all-gather = f32[2048,64]{1,0:T(8,128)S(1)} all-gather(f32[64,64]{1,0:T(8,128)S(1)} %fusion.14), channel_id=2, replica_groups=mesh['space'=32,'tm'=8] {'space'}, dimensions={0}, use_global_device_ids=true | all-gather | bytes 540672 | tf_op jit(solution)/shard_map/all_gather | solution.py:32
  67.8 4.2 fusion.4
  73.8 126.4 %psum.21 = f32[1,32,32]{1,2,0:T(8,128)S(1)} all-reduce(f32[1,32,32]{1,2,0:T(8,128)S(1)} %convolution_bitcast_fusion.5), channel_id=1, replica_groups=mesh['space'=32,'tm'=8] {'space'}, use_global_device_ids=true, to_apply=%region_1.2 | all-reduce | flops 1024 | bytes 8192 | tf_op jit(solution)/shard_map/psum | solution.py:40
  200.3 2.9 custom-call.16
  204.5 2.4 custom-call.17
  208.1 3.3 fusion.62
  211.4 3.4 collective-permute-start.3
  214.8 85.8 %collective-permute-done.3 = f32[32,16,1024]{2,0,1:T(8,128)S(1)} collective-permute-done((f32[32,16,1024]{2,0,1:T(8,128)}, f32[32,16,1024]{2,0,1:T(8,128)S(1)}, u32[]{:S(2)}, u32[]{:S(2)}) %collective-permute-start.3) | collective-permute-done | bytes 2097184 | tf_op jit(solution)/shard_map/ppermute | solution.py:26
  300.6 2.1 broadcast_select_fusion.1
  302.7 3.4 fusion.15
  306.1 22.0 %all-gather.1 = f32[2048,64]{1,0:T(8,128)S(1)} all-gather(f32[64,64]{1,0:T(8,128)S(1)} %fusion.15), channel_id=3, replica_groups=mesh['space'=32,'tm'=8] {'space'}, dimensions={0}, use_global_device_ids=true | all-gather | bytes 540672 | tf_op jit(solution)/shard_map/all_gather | solution.py:32
  329.0 4.2 fusion.2
  335.0 126.4 %psum.22 = f32[1,32,32]{1,2,0:T(8,128)S(1)} all-reduce(f32[1,32,32]{1,2,0:T(8,128)S(1)} %convolution_bitcast_fusion.3), channel_id=1, replica_groups=mesh['space'=32,'tm'=8] {'space'}, use_global_device_ids=true, to_apply=%region_5.8 | all-reduce | flops 1024 | bytes 8192 | tf_op jit(solution)/shard_map/psum | solution.py:40
  461.5 2.9 custom-call.18
  465.7 2.4 custom-call.19
  468.5 3.3 fusion.63
  471.7 6.9 collective-permute-start.4
  480.2 84.9 %collective-permute-done.4 = f32[32,16,1024]{2,0,1:T(8,128)S(1)} collective-permute-done((f32[32,16,1024]{2,0,1:T(8,128)}, f32[32,16,1024]{2,0,1:T(8,128)S(1)}, u32[]{:S(2)}, u32[]{:S(2)}) %collective-permute-start.4) | collective-permute-done | bytes 2097184 | tf_op jit(solution)/shard_map/ppermute | solution.py:26
  565.1 2.1 broadcast_select_fusion.3
  567.3 3.4 fusion.16
  570.7 22.0 %all-gather.2 = f32[2048,64]{1,0:T(8,128)S(1)} all-gather(f32[64,64]{1,0:T(8,128)S(1)} %fusion.16), channel_id=4, replica_groups=mesh['space'=32,'tm'=8] {'space'}, dimensions={0}, use_global_device_ids=true | all-gather | bytes 540672 | tf_op jit(solution)/shard_map/all_gather | solution.py:32
  593.5 4.2 fusion
  599.6 126.6 %psum.23 = f32[1,32,32]{1,2,0:T(8,128)S(1)} all-reduce(f32[1,32,32]{1,2,0:T(8,128)S(1)} %convolution_bitcast_fusion.1), channel_id=1, replica_groups=mesh['space'=32,'tm'=8] {'space'}, use_global_device_ids=true, to_apply=%region_7.10 | all-reduce | flops 1024 | bytes 8192 | tf_op jit(solution)/shard_map/psum | solution.py:40
  726.3 2.9 custom-call.20
  730.5 2.4 custom-call.21
  (58 shorter events, 22.7 us)
Async XLA Ops:
  3.4 6.9 collective-permute-start.1
  6.4 9.1 %collective-permute-start = (bf16[32,2,2,1024]{3,0,2,1:T(8,128)(2,1)S(1)}, bf16[32,2,2,1024]{3,0,2,1:T(8,128)(2,1)S(1)}, u32[]{:S(2)}, u32[]{:S(2)}) collective-permute-start(bf16[32,2,2,1024]{3,0,2,1:T(8,128)(2,1)S(1)} %get-tuple-element.26), channel_id=1, source_target_pairs={{0,8},{8,16},{16,24},{24,32},{32,40},{40,48},{48,56},{56,64},{64,7... | collective-permute-start | bytes 786440 | tf_op jit(solution)/shard_map/ppermute | solution.py:15
  20.5 17.7 %collective-permute-start.2 = (bf16[32,16,1024]{2,0,1:T(8,128)(2,1)S(1)}, bf16[32,16,1024]{2,0,1:T(8,128)(2,1)S(1)}, u32[]{:S(2)}, u32[]{:S(2)}) collective-permute-start(bf16[32,16,1024]{2,0,1:T(8,128)(2,1)S(1)} %fusion.9), channel_id=1, source_target_pairs={{0,1},{1,0},{2,3},{3,2},{4,5},{5,4},{6,7},{7,6},{8,9},{9,8},{10,11... | collective-permute-start | bytes 3145736 | tf_op jit(solution)/shard_map/ppermute | solution.py:26
  38.8 3.4 copy-start
  38.8 3.4 copy-start.1
  211.4 89.2 %collective-permute-start.3 = (f32[32,16,1024]{2,0,1:T(8,128)}, f32[32,16,1024]{2,0,1:T(8,128)S(1)}, u32[]{:S(2)}, u32[]{:S(2)}) collective-permute-start(f32[32,16,1024]{2,0,1:T(8,128)} %fusion.62), channel_id=1, source_target_pairs={{0,2},{1,3},{2,0},{3,1},{4,6},{5,7},{6,4},{7,5},{8,10},{9,11},{10,... | collective-permute-start | bytes 6291464 | tf_op jit(solution)/shard_map/ppermute | solution.py:26
  302.7 3.4 copy-start.4
  302.7 3.4 copy-start.5
  471.7 93.4 %collective-permute-start.4 = (f32[32,16,1024]{2,0,1:T(8,128)}, f32[32,16,1024]{2,0,1:T(8,128)S(1)}, u32[]{:S(2)}, u32[]{:S(2)}) collective-permute-start(f32[32,16,1024]{2,0,1:T(8,128)} %fusion.63), channel_id=1, source_target_pairs={{0,4},{1,5},{2,6},{3,7},{4,0},{5,1},{6,2},{7,3},{8,12},{9,13},{10,... | collective-permute-start | bytes 6291464 | tf_op jit(solution)/shard_map/ppermute | solution.py:26
  567.3 3.4 copy-start.2
  567.3 3.4 copy-start.3
